TPU v7x, 256 devices: a whole 4x4x8 slice. The times are simulated.
256 devices in a mesh: freq: 16 (over y, x), tile: 16 (over z, core).
Axes of the slice: x: 4, y: 4, z: 8, core: 2. Of those that a mesh axis runs over, the one named last changes fastest.
Arguments:
- x_field: bfloat16 [16, 2, 10240, 256], P('freq', None, 'tile'), may hold values from -6 to 6
- data: bfloat16 [16, 2, 10240, 256], P('freq', None, 'tile'), may hold values from -6 to 6
- u_bases: bfloat16 [16, 16, 16, 128, 2, 640], P('freq', 'tile'), may hold values from -0.15625 to 0.15625
- v_bases: bfloat16 [16, 16, 16, 128, 2, 640], P('freq', None, 'tile'), may hold values from -0.15625 to 0.15625
- ranks: int32 [16, 16, 16], P('freq'), may hold values from 49 to 96, as said below
- onset: int32 [10240, 256], P(('tile', 'freq')), may hold values from 0 to 15
Outputs:
- gradient: float32 [32, 10240, 256], P(None, ('tile', 'freq'))
Inputs may be any that keep to these rules, and one draw needn't show every extreme that they name: ranks[f,r,c] is the rank of tile (r, c) at frequency f; it is at most 96, and equal to 96 for some tile of every frequency.
All inputs are finite; a program needn't handle non-finite values.
Results may differ from a plain program's by a relative error of at most 0.0055.
Values may be sent and summed in bfloat16 or wider, within the bound.
A program may use at most 64 MiB of HBM per device.

v0:
```python
import math

import jax
import jax.numpy as jnp
from jax import lax
from jax.sharding import PartitionSpec as P

RMAX = 96


PRECISE = lax.Precision.HIGHEST


def conj_apply(factors, vectors):
    partner = jnp.stack([vectors[1], -vectors[0]])
    stacked = jnp.stack([vectors, partner], axis=2)
    return jnp.einsum("nkps,psov->nkov", factors, stacked, preferred_element_type=jnp.float32)


def apply_factors(factors, weights):
    real_part = weights[:, :, 0]
    imag_part = weights[:, :, 1]
    blended = jnp.stack(
        [jnp.stack([real_part, imag_part], axis=2), jnp.stack([-imag_part, real_part], axis=2)],
        axis=2,
    )
    return jnp.einsum("nkps,nkpov->osv", factors, blended, preferred_element_type=jnp.float32)


def body(x_field, data, u_bases, v_bases, ranks, onset):
    position = lax.axis_index("tile")
    extent = RMAX
    row_factors = u_bases[0, 0, :, :extent]
    column_factors = v_bases[0, :, 0, :extent]
    rank_table = ranks[0]
    column_ranks = lax.dynamic_index_in_dim(rank_table, position, 1, keepdims=False)
    row_ranks = lax.dynamic_index_in_dim(rank_table, position, 0, keepdims=False)
    levels = jnp.arange(extent, dtype=jnp.int32)
    column_mask = (levels[None, :] < column_ranks[:, None]).astype(jnp.float32)
    row_mask = (levels[None, :] < row_ranks[:, None]).astype(jnp.float32)
    coeffs = (conj_apply(column_factors, x_field[0]) * column_mask[:, :, None, None]).astype(
        jnp.bfloat16
    )
    predicted = apply_factors(
        row_factors, lax.all_to_all(coeffs, "tile", split_axis=0, concat_axis=0, tiled=True)
    )
    residual = (predicted - data[0].astype(jnp.float32)).astype(jnp.bfloat16)
    adjoint = (conj_apply(row_factors, residual) * row_mask[:, :, None, None]).astype(jnp.bfloat16)
    spectrum = apply_factors(
        column_factors, lax.all_to_all(adjoint, "tile", split_axis=0, concat_axis=0, tiled=True)
    ).astype(jnp.bfloat16)
    freq_count = lax.axis_size("freq")
    time_count = 2 * freq_count
    moments = jnp.arange(time_count, dtype=jnp.int32)
    orders = jnp.arange(1, freq_count + 1, dtype=jnp.int32)
    phases = moments[:, None] * orders[None, :] % time_count
    angles = 2.0 * math.pi / time_count * phases.astype(jnp.float32)
    cosine = jnp.cos(angles)
    sine_part = jnp.sin(angles)
    scaling = 1.0 / math.sqrt(freq_count)
    received = lax.all_to_all(spectrum[None], "freq", split_axis=2, concat_axis=0, tiled=True)
    stations = received.shape[2]
    column_count = received.shape[3]
    real_part = received[:, 0].astype(jnp.float32).reshape(freq_count, -1)
    imag_part = received[:, 1].astype(jnp.float32).reshape(freq_count, -1)
    traces = jnp.dot(cosine, real_part, precision=PRECISE) - jnp.dot(
        sine_part, imag_part, precision=PRECISE
    )
    traces = (traces * scaling).reshape(time_count, stations, column_count)
    return jnp.where(moments[:, None, None] >= onset[None], traces, jnp.float32(0.0))


def solution(mesh):
    in_specs = (
        P("freq", None, "tile", None),
        P("freq", None, "tile", None),
        P("freq", "tile", None, None, None, None),
        P("freq", None, "tile", None, None, None),
        P("freq", None, None),
        P(("tile", "freq"), None),
    )
    out_specs = P(None, ("tile", "freq"), None)
    return jax.shard_map(body, mesh=mesh, in_specs=in_specs, out_specs=out_specs, check_vma=False)
```

profile of v0, /device:TPU:1, one launch (start us, length us, event | category | flops | bytes accessed | tf_op | source)
XLA Modules:
  0.0 140.8 jit_solution(14404263094056278529)
XLA Ops:
  0.0 0.7 copy-done
  0.7 0.2 dynamic-slice_reduce_fusion
  1.0 1.1 slice_bitcast_fusion
  2.1 5.0 %slice.45 = bf16[1,16,1,96,2,640]{5,4,3,2,1,0:T(2,128)(2,1)S(1)} slice(bf16[1,16,1,128,2,640]{5,4,3,2,1,0:T(2,128)(2,1)} %param.9), slice={[0:1], [0:16], [0:1], [0:96], [0:2], [0:640]} | slice | bytes 7864320 | tf_op jit(solution)/shard_map/slice | solution.py:34
  7.2 2.2 %fusion.19 = bf16[16,96,2,256]{3,1,0,2:T(8,128)(2,1)S(1)} fusion(f32[16,96]{1,0:T(8,128)S(1)} %fusion.62, bf16[1,16,1,96,2,640]{5,4,3,2,1,0:T(2,128)(2,1)S(1)} %slice.45, bf16[2,640,1,256]{3,1,0,2:T(8,128)(2,1)S(1)} %maximum_bitcast_fusion.6, bf16[2,640,1,256]{3,1,0,2:T(8,128)(2,1)S(1)} %bitcast.142), kind=kOutput, calls=%fused_computation.24 | convolution fusion | flops 2017460224 | bytes 6821888 | tf_op jit(solution)/shard_map/nkps,psov->nkov/dot_general | solution.py:17
  9.5 1.4 copy.21
  10.8 10.0 %all-to-all-start = ((bf16[16,96,2,256]{3,1,2,0:T(8,128)(2,1)}), bf16[16,96,2,256]{3,1,2,0:T(8,128)(2,1)S(1)}, u32[]{:S(2)}, u32[]{:S(2)}) async-start(bf16[16,96,2,256]{3,1,2,0:T(8,128)(2,1)} %copy.21), calls=%async_computation | async-start | bytes 3145728 | tf_op jit(solution)/shard_map/all_to_all | solution.py:45
  20.8 6.9 %slice.48 = bf16[1,1,16,96,2,640]{5,4,3,2,1,0:T(2,128)(2,1)} slice(bf16[1,1,16,128,2,640]{5,4,3,2,1,0:T(2,128)(2,1)} %param.8), slice={[0:1], [0:1], [0:16], [0:96], [0:2], [0:640]} | slice | bytes 7864320 | tf_op jit(solution)/shard_map/slice | solution.py:33
  27.8 0.3 copy.26
  28.1 31.1 %all-to-all-done = bf16[16,96,2,256]{3,1,2,0:T(8,128)(2,1)S(1)} async-done(((bf16[16,96,2,256]{3,1,2,0:T(8,128)(2,1)}), bf16[16,96,2,256]{3,1,2,0:T(8,128)(2,1)S(1)}, u32[]{:S(2)}, u32[]{:S(2)}) %all-to-all-start) | async-done | bytes 1572896 | tf_op jit(solution)/shard_map/all_to_all | solution.py:45
  59.2 0.1 copy.92
  59.4 0.1 slice_negate_fusion.1
  59.5 0.1 maximum_bitcast_fusion
  59.6 1.8 %copy-done.3 = bf16[1,1,16,96,2,640]{5,4,3,2,1,0:T(2,128)(2,1)S(1)} copy-done((bf16[1,1,16,96,2,640]{5,4,3,2,1,0:T(2,128)(2,1)S(1)}, bf16[1,1,16,96,2,640]{5,4,3,2,1,0:T(2,128)(2,1)}, u32[]{:S(2)}) %copy-start.3) | copy-done | bytes 3932184
  61.5 2.7 %fusion.39 = bf16[2,640,256]{1,2,0:T(8,128)(2,1)S(1)} fusion(bf16[1,1,16,96,2,640]{5,4,3,2,1,0:T(2,128)(2,1)S(1)} %copy-done.3, bf16[16,96,1,2,256]{4,1,0,3,2:T(8,128)(2,1)S(1)} %maximum_bitcast_fusion, bf16[16,96,1,2,256]{4,1,0,3,2:T(8,128)(2,1)S(1)} %bitcast.134, bf16[1,2,640,256]{2,3,1,0:T(8,128)(2,1)S(1)} %copy.26), kind=kOutput, calls=%fused_computation.30 | convolution fusion | flops 2015821824 | bytes 8388608 | tf_op jit(solution)/shard_map/nkps,nkpov->osv/dot_general | solution.py:27
  64.3 2.2 %fusion.20 = bf16[16,96,2,256]{3,1,0,2:T(8,128)(2,1)S(1)} fusion(f32[16,96]{1,0:T(8,128)S(1)} %fusion.63, bf16[1,1,16,96,2,640]{5,4,3,2,1,0:T(2,128)(2,1)S(1)} %copy-done.3, bf16[2,640,1,256]{1,3,0,2:T(8,128)(2,1)S(1)} %maximum_bitcast_fusion.7, bf16[2,640,1,256]{1,3,0,2:T(8,128)(2,1)S(1)} %bitcast.143), kind=kOutput, calls=%fused_computation.25 | convolution fusion | flops 2017460224 | bytes 6821888 | tf_op jit(solution)/shard_map/nkps,psov->nkov/dot_general | solution.py:17
  66.6 0.1 copy.29
  66.7 43.8 %all_to_all.28 = bf16[16,96,2,256]{3,1,2,0:T(8,128)(2,1)S(1)} all-to-all(bf16[16,96,2,256]{3,1,2,0:T(8,128)(2,1)S(1)} %copy.29), channel_id=1, replica_groups=mesh['freq'=16,'tile'=16] {'tile'}, dimensions={0} | all-to-all | bytes 3145728 | tf_op jit(solution)/shard_map/all_to_all | solution.py:50
  110.6 0.1 copy.91
  110.7 0.1 slice_negate_fusion
  110.8 0.1 maximum_bitcast_fusion.1
  111.0 1.8 %copy-done.2 = bf16[1,16,1,96,2,640]{5,4,3,2,1,0:T(2,128)(2,1)S(1)} copy-done((bf16[1,16,1,96,2,640]{5,4,3,2,1,0:T(2,128)(2,1)S(1)}, bf16[1,16,1,96,2,640]{5,4,3,2,1,0:T(2,128)(2,1)}, u32[]{:S(2)}) %copy-start.2) | copy-done | bytes 3932184
  112.8 2.7 %fusion.46 = bf16[1,2,640,256]{2,3,1,0:T(8,128)(2,1)S(1)} fusion(bf16[1,16,1,96,2,640]{5,4,3,2,1,0:T(2,128)(2,1)S(1)} %copy-done.2, bf16[16,96,1,2,256]{4,1,0,3,2:T(8,128)(2,1)S(1)} %maximum_bitcast_fusion.1, bf16[16,96,1,2,256]{4,1,0,3,2:T(8,128)(2,1)S(1)} %bitcast.135), kind=kOutput, calls=%fused_computation.39 | convolution fusion | flops 2015166464 | bytes 7733248 | tf_op jit(solution)/shard_map/nkps,nkpov->osv/dot_general | solution.py:27
  115.5 1.8 %copy.34 = bf16[1,2,640,256]{3,1,0,2:T(2,128)(2,1)} copy(bf16[1,2,640,256]{2,3,1,0:T(8,128)(2,1)S(1)} %fusion.46) | data formatting | bytes 1310720 | tf_op jit(solution)/shard_map/broadcast_in_dim | solution.py:61
  117.3 6.8 %all-to-all-start.2 = ((bf16[1,2,640,256]{3,1,0,2:T(2,128)(2,1)}), bf16[1,2,640,256]{3,1,0,2:T(2,128)(2,1)S(1)}, u32[]{:S(2)}, u32[]{:S(2)}) async-start(bf16[1,2,640,256]{3,1,0,2:T(2,128)(2,1)} %copy.34), calls=%async_computation.2 | async-start | bytes 1310720 | tf_op jit(solution)/shard_map/all_to_all | solution.py:61
  124.1 12.9 %all-to-all-done.2 = bf16[1,2,640,256]{3,1,0,2:T(2,128)(2,1)S(1)} async-done(((bf16[1,2,640,256]{3,1,0,2:T(2,128)(2,1)}), bf16[1,2,640,256]{3,1,0,2:T(2,128)(2,1)S(1)}, u32[]{:S(2)}, u32[]{:S(2)}) %all-to-all-start.2) | async-done | bytes 655392 | tf_op jit(solution)/shard_map/all_to_all | solution.py:61
  137.0 0.1 copy.35
  137.3 0.7 fusion.55
  138.0 0.8 fusion
  138.8 0.4 copy.54
  139.2 0.4 copy-done.6
  139.6 1.2 bitcast_select_fusion
  (20 shorter events, 0.5 us)
Async XLA Ops:
  0.0 0.7 copy-start
  2.1 5.2 %copy-start.4 = (bf16[1,2,640,256]{3,2,1,0:T(8,128)(2,1)S(1)}, bf16[1,2,640,256]{3,2,1,0:T(8,128)(2,1)}, u32[]{:S(2)}) copy-start(bf16[1,2,640,256]{3,2,1,0:T(8,128)(2,1)} %param.6) | copy-start | bytes 1966084
  7.1 2.3 %copy-start.1 = (bf16[1,16,1,96,2,640]{5,4,3,2,1,0:T(2,128)(2,1)}, bf16[1,16,1,96,2,640]{5,4,3,2,1,0:T(2,128)(2,1)S(1)}, u32[]{:S(2)}) copy-start(bf16[1,16,1,96,2,640]{5,4,3,2,1,0:T(2,128)(2,1)S(1)} %slice.45) | copy-start | bytes 11796484
  10.8 48.4 %all-to-all-start = ((bf16[16,96,2,256]{3,1,2,0:T(8,128)(2,1)}), bf16[16,96,2,256]{3,1,2,0:T(8,128)(2,1)S(1)}, u32[]{:S(2)}, u32[]{:S(2)}) async-start(bf16[16,96,2,256]{3,1,2,0:T(8,128)(2,1)} %copy.21), calls=%async_computation | async-start | bytes 3145728 | tf_op jit(solution)/shard_map/all_to_all | solution.py:45
  20.8 6.9 %copy-start.5 = (bf16[1,2,640,256]{3,2,1,0:T(8,128)(2,1)S(1)}, bf16[1,2,640,256]{3,2,1,0:T(8,128)(2,1)}, u32[]{:S(2)}) copy-start(bf16[1,2,640,256]{3,2,1,0:T(8,128)(2,1)} %param.7) | copy-start | bytes 1966084
  59.4 2.1 %copy-start.3 = (bf16[1,1,16,96,2,640]{5,4,3,2,1,0:T(2,128)(2,1)S(1)}, bf16[1,1,16,96,2,640]{5,4,3,2,1,0:T(2,128)(2,1)}, u32[]{:S(2)}) copy-start(bf16[1,1,16,96,2,640]{5,4,3,2,1,0:T(2,128)(2,1)} %slice.48) | copy-start | bytes 11796484
  110.7 2.1 %copy-start.2 = (bf16[1,16,1,96,2,640]{5,4,3,2,1,0:T(2,128)(2,1)S(1)}, bf16[1,16,1,96,2,640]{5,4,3,2,1,0:T(2,128)(2,1)}, u32[]{:S(2)}) copy-start(bf16[1,16,1,96,2,640]{5,4,3,2,1,0:T(2,128)(2,1)} %copy-done.1) | copy-start | bytes 11796484
  117.3 19.7 %all-to-all-start.2 = ((bf16[1,2,640,256]{3,1,0,2:T(2,128)(2,1)}), bf16[1,2,640,256]{3,1,0,2:T(2,128)(2,1)S(1)}, u32[]{:S(2)}, u32[]{:S(2)}) async-start(bf16[1,2,640,256]{3,1,0,2:T(2,128)(2,1)} %copy.34), calls=%async_computation.2 | async-start | bytes 1310720 | tf_op jit(solution)/shard_map/all_to_all | solution.py:61
  138.8 0.8 copy-start.6
where the time goes:
time: 141 us
  waiting for transfers between devices  44 us (31%)
  blocking collectives  43.8 us (31%)
  local copies, waits for them, and re-layouts  21.4 us (15%)
  starting transfers between devices  16.7 us (12%)
  matrix products  11.4 us (8%)
  other arithmetic  3.14 us (2%)
    all_to_all x1, blocking collectives, body(): lax.all_to_all(adjoint, 'tile', split_axis=0, concat_axis=0, tiled=True)  43.8 us
    all_to_all x1, waiting for transfers between devices, body(): lax.all_to_all(coeffs, 'tile', split_axis=0, concat_axis=0, tiled=True)  31.1 us
    all_to_all x1, waiting for transfers between devices, body(): lax.all_to_all(spectrum[None], 'freq', split_axis=2, concat_axis=0, tiled...  12.9 us
    all_to_all x1, starting transfers between devices, body(): lax.all_to_all(coeffs, 'tile', split_axis=0, concat_axis=0, tiled=True)  9.98 us
    slice x1, local copies, waits for them, and re-layouts, body(): row_factors = u_bases[0, 0, :, :extent]  6.93 us
    all_to_all x1, starting transfers between devices, body(): lax.all_to_all(spectrum[None], 'freq', split_axis=2, concat_axis=0, tiled...  6.75 us
    unnamed x18, local copies, waits for them, and re-layouts  5.57 us
    dot_general x2, matrix products, apply_factors(): jnp.einsum('nkps,nkpov->osv', factors, blended, preferred_element_type=jn...  5.44 us
  transfers between devices with their start and end apart: 2, of which 2 were waited for; matrix products, arithmetic and copies ran while one was open for 5% of the time, Pallas kernels for 0%

commit v1 on v0

v1 whole, which is shorter than its diff:
```python
import functools
import math

import jax
import jax.numpy as jnp
from jax import lax
from jax.experimental import pallas as pl
from jax.experimental.pallas import tpu as pltpu
from jax.sharding import PartitionSpec as P

RMAX = 96
HALF = 128
MESH = pl.DeviceIdType.MESH
CONTRACT_ROWS = (((0,), (0,)), ((), ()))


def hop(slot):
    step = slot // 2
    quarter = step // 2
    odd = step % 2
    return 4 + quarter - odd * (2 * quarter + 1), (slot + slot // 14) % 2


def tile_at(position, slot, sign):
    chips, cores = hop(slot)
    return (position // 2 + sign * chips + 8) % 8 * 2 + (position % 2 + cores) % 2


def freq_at(position, slot):
    return (position // 4 + slot // 4) % 4 * 4 + (position % 4 + slot % 4) % 4


def exchange_kernel(
    ranks_ref, x_hbm, d_hbm, u_hbm, v_hbm, out_ref,
    x_mat, x_rot, d_mat, v_raw, u_raw, v_mat, u_mat, total,
    c_send, c_recv, a_send, a_recv, f_send, f_recv,
    load_sem, v_sem, u_sem, c_sems, a_sems, f_sems, out_sem,
):
    freq = lax.axis_index("freq")
    tile = lax.axis_index("tile")
    barrier = pltpu.get_barrier_semaphore()

    def greet_tile(slot, carry):
        pl.semaphore_signal(barrier, inc=1, device_id=(freq, tile_at(tile, slot, 1)), device_id_type=MESH)
        return carry

    def greet_freq(slot, carry):
        pl.semaphore_signal(barrier, inc=1, device_id=(freq_at(freq, slot), tile), device_id_type=MESH)
        return carry

    lax.fori_loop(0, 15, greet_tile, 0)
    lax.fori_loop(1, 16, greet_freq, 0)

    def field_copy(source, target, half, part, index):
        return pltpu.make_async_copy(
            source.at[0, part, :, pl.ds(half * HALF, HALF)],
            target.at[half, :, pl.ds(part * HALF, HALF)],
            load_sem.at[index, half, part],
        )

    def v_copy(slot):
        return pltpu.make_async_copy(
            v_hbm.at[0, tile_at(tile, slot, 1), 0, pl.ds(0, RMAX)], v_raw.at[slot], v_sem.at[slot]
        )

    def u_copy(slot):
        return pltpu.make_async_copy(
            u_hbm.at[0, 0, tile_at(tile, slot, -1), pl.ds(0, RMAX)], u_raw.at[slot], u_sem.at[slot]
        )

    def start_v(slot, carry):
        v_copy(slot).start()
        return carry

    def start_u(slot, carry):
        u_copy(slot).start()
        return carry

    field_copy(x_hbm, x_mat, 0, 0, 0).start()
    field_copy(x_hbm, x_mat, 0, 1, 0).start()
    lax.fori_loop(0, 16, start_v, 0)
    field_copy(x_hbm, x_mat, 1, 0, 0).start()
    field_copy(x_hbm, x_mat, 1, 1, 0).start()
    lax.fori_loop(0, 16, start_u, 0)
    for half in range(2):
        for part in range(2):
            field_copy(d_hbm, d_mat, half, part, 1).start()

    rows = lax.broadcasted_iota(jnp.int32, (2 * RMAX, 2 * RMAX), 0)
    columns = lax.broadcasted_iota(jnp.int32, (2 * RMAX, 2 * RMAX), 1)
    wanted = jnp.where(rows < RMAX, 2 * rows, 2 * (rows - RMAX) + 1)
    separate = jnp.where(columns == wanted, 1.0, 0.0).astype(jnp.bfloat16)
    levels = lax.broadcasted_iota(jnp.int32, (RMAX, 2 * HALF), 0)

    def separated(raw):
        interleaved = raw.reshape(2 * RMAX, raw.shape[-1])
        return jnp.dot(separate, interleaved, preferred_element_type=jnp.float32).astype(jnp.bfloat16)

    def rotated(field):
        return jnp.concatenate([field[:, HALF:], -field[:, :HALF]], axis=1)

    def conj_apply(basis, slot, field, partner, rank):
        value = jnp.dot(basis[slot, pl.ds(0, RMAX)], field, preferred_element_type=jnp.float32)
        value += jnp.dot(basis[slot, pl.ds(RMAX, RMAX)], partner, preferred_element_type=jnp.float32)
        return jnp.where(levels < rank, value, 0.0).astype(jnp.bfloat16)

    def apply_basis(basis, slot, weights):
        partner = jnp.concatenate([-weights[:, HALF:], weights[:, :HALF]], axis=1)
        blended = jnp.concatenate([weights, partner], axis=0)
        return lax.dot_general(basis[slot], blended, CONTRACT_ROWS, preferred_element_type=jnp.float32)

    def c_copy(half, slot):
        return pltpu.make_async_remote_copy(
            src_ref=c_send.at[half, slot], dst_ref=c_recv.at[half, slot],
            send_sem=c_sems.at[0, half, slot], recv_sem=c_sems.at[1, half, slot],
            device_id=(freq, tile_at(tile, slot, 1)), device_id_type=MESH,
        )

    def a_copy(half, slot):
        return pltpu.make_async_remote_copy(
            src_ref=a_send.at[half, slot], dst_ref=a_recv.at[half, slot],
            send_sem=a_sems.at[0, half, slot], recv_sem=a_sems.at[1, half, slot],
            device_id=(freq, tile_at(tile, slot, -1)), device_id_type=MESH,
        )

    def f_copy(half, slot):
        peer = freq_at(freq, slot)
        return pltpu.make_async_remote_copy(
            src_ref=f_send.at[half, peer], dst_ref=f_recv.at[half, freq],
            send_sem=f_sems.at[0, half, slot], recv_sem=f_sems.at[1, half, slot],
            device_id=(peer, tile), device_id_type=MESH,
        )

    def coefficients(half, slot):
        rank = ranks_ref[0, tile_at(tile, slot, 1), tile]
        return conj_apply(v_mat, slot, x_mat[half], x_rot[half], rank)

    def prepare_v(slot):
        v_copy(slot).wait()
        v_mat[slot] = separated(v_raw[slot])

    def wait_field(half, index, source, target):
        for part in range(2):
            field_copy(source, target, half, part, index).wait()

    wait_field(0, 0, x_hbm, x_mat)
    x_rot[0] = rotated(x_mat[0])
    prepare_v(0)
    c_send[0, 0] = coefficients(0, 0)
    pl.semaphore_wait(barrier, 30)
    c_copy(0, 0).start()

    def send_first(slot, carry):
        prepare_v(slot)
        c_send[0, slot] = coefficients(0, slot)
        c_copy(0, slot).start()
        return carry

    lax.fori_loop(1, 15, send_first, 0)
    prepare_v(15)
    c_recv[0, 15] = coefficients(0, 15)

    wait_field(1, 0, x_hbm, x_mat)
    x_rot[1] = rotated(x_mat[1])

    def send_second(slot, carry):
        c_send[1, slot] = coefficients(1, slot)
        c_copy(1, slot).start()
        return carry

    lax.fori_loop(0, 15, send_second, 0)
    c_recv[1, 15] = coefficients(1, 15)

    def prepare_u(slot, carry):
        u_copy(slot).wait()
        u_mat[slot] = separated(u_raw[slot])
        return carry

    lax.fori_loop(0, 16, prepare_u, 0)

    for half in range(2):
        wait_field(half, 1, d_hbm, d_mat)
        total[...] = apply_basis(u_mat, 15, c_recv[half, 15]) - d_mat[half].astype(jnp.float32)

        def predict(slot, carry):
            c_copy(half, slot).wait_recv()
            total[...] += apply_basis(u_mat, slot, c_recv[half, slot])
            return carry

        lax.fori_loop(0, 15, predict, 0)
        x_mat[half] = total[...].astype(jnp.bfloat16)
        x_rot[half] = rotated(x_mat[half])

        def adjoint(slot):
            rank = ranks_ref[0, tile, tile_at(tile, slot, -1)]
            return conj_apply(u_mat, slot, x_mat[half], x_rot[half], rank)

        def send_adjoint(slot, carry):
            a_send[half, slot] = adjoint(slot)
            a_copy(half, slot).start()
            return carry

        lax.fori_loop(0, 15, send_adjoint, 0)
        a_recv[half, 15] = adjoint(15)

    for half in range(2):
        total[...] = apply_basis(v_mat, 15, a_recv[half, 15])

        def gather(slot, carry):
            a_copy(half, slot).wait_recv()
            total[...] += apply_basis(v_mat, slot, a_recv[half, slot])
            return carry

        lax.fori_loop(0, 15, gather, 0)
        for peer in range(16):
            f_send[half, peer] = total[pl.ds(peer * 40, 40)].astype(jnp.bfloat16)

        def send_spectrum(slot, carry):
            f_copy(half, slot).start()
            return carry

        lax.fori_loop(1, 16, send_spectrum, 0)
        own = pltpu.make_async_copy(f_send.at[half, freq], f_recv.at[half, freq], out_sem.at[half])
        own.start()
        own.wait()

    for half in range(2):

        def finish_freq(slot, carry):
            f_copy(half, slot).wait()
            return carry

        lax.fori_loop(1, 16, finish_freq, 0)

        def finish_tile(slot, carry):
            c_copy(half, slot).wait_send()
            a_copy(half, slot).wait_send()
            return carry

        lax.fori_loop(0, 15, finish_tile, 0)
    out = pltpu.make_async_copy(f_recv, out_ref, out_sem.at[0])
    out.start()
    out.wait()


def traces_kernel(s_ref, onset_ref, g_ref):
    count = s_ref.shape[1]
    period = 2 * count
    scale = 1.0 / math.sqrt(count)

    def weighted(terms):
        value = None
        for factor, term in terms:
            if abs(factor) < 1e-12:
                continue
            product = term * jnp.float32(factor)
            value = product if value is None else value + product
        return jnp.zeros((8, HALF), jnp.float32) if value is None else value

    for half in range(2):
        lanes = pl.ds(half * HALF, HALF)
        for block in range(s_ref.shape[2] // 8):
            rows = pl.ds(block * 8, 8)
            onset = onset_ref[rows, lanes]
            real = [s_ref[half, f, rows, pl.ds(0, HALF)].astype(jnp.float32) for f in range(count)]
            imag = [s_ref[half, f, rows, pl.ds(HALF, HALF)].astype(jnp.float32) for f in range(count)]

            def store(time, value):
                g_ref[time, rows, lanes] = jnp.where(onset <= time, value, 0.0)

            for t in range(count // 2 + 1):
                cosine = [scale * math.cos(2 * math.pi * (((f + 1) * t) % period) / period) for f in range(count)]
                sine = [scale * math.sin(2 * math.pi * (((f + 1) * t) % period) / period) for f in range(count)]
                odd_c = weighted([(cosine[f], real[f]) for f in range(0, count, 2)])
                even_c = weighted([(cosine[f], real[f]) for f in range(1, count, 2)])
                odd_s = weighted([(sine[f], imag[f]) for f in range(0, count, 2)])
                even_s = weighted([(sine[f], imag[f]) for f in range(1, count, 2)])
                store(t, (even_c + odd_c) - (even_s + odd_s))
                if t < count - t:
                    store(count - t, (even_c - odd_c) + (even_s - odd_s))
                if 0 < t:
                    store(period - t, (even_c + odd_c) + (even_s + odd_s))
                    if count + t < period - t:
                        store(count + t, (even_c - odd_c) - (even_s - odd_s))


def body(x_field, data, u_bases, v_bases, ranks, onset):
    stations, points = x_field.shape[2:]
    tiles = 16
    count = lax.axis_size("freq")
    share = stations // count
    bf16, f32 = jnp.bfloat16, jnp.float32
    anywhere = pl.BlockSpec(memory_space=pl.ANY)
    dma = pltpu.SemaphoreType.DMA
    spectra = pl.pallas_call(
        exchange_kernel,
        name="exchange",
        out_shape=jax.ShapeDtypeStruct((2, count, share, 2 * HALF), bf16),
        in_specs=[pl.BlockSpec(memory_space=pltpu.SMEM)] + [anywhere] * 4,
        out_specs=anywhere,
        scratch_shapes=[
            pltpu.VMEM((2, stations, 2 * HALF), bf16),
            pltpu.VMEM((2, stations, 2 * HALF), bf16),
            pltpu.VMEM((2, stations, 2 * HALF), bf16),
            pltpu.VMEM((tiles, RMAX, 2, stations), bf16),
            pltpu.VMEM((tiles, RMAX, 2, stations), bf16),
            pltpu.VMEM((tiles, 2 * RMAX, stations), bf16),
            pltpu.VMEM((tiles, 2 * RMAX, stations), bf16),
            pltpu.VMEM((stations, 2 * HALF), f32),
            pltpu.VMEM((2, tiles, RMAX, 2 * HALF), bf16),
            pltpu.VMEM((2, tiles, RMAX, 2 * HALF), bf16),
            pltpu.VMEM((2, tiles, RMAX, 2 * HALF), bf16),
            pltpu.VMEM((2, tiles, RMAX, 2 * HALF), bf16),
            pltpu.VMEM((2, count, share, 2 * HALF), bf16),
            pltpu.VMEM((2, count, share, 2 * HALF), bf16),
            dma((2, 2, 2)),
            dma((tiles,)),
            dma((tiles,)),
            dma((2, 2, tiles)),
            dma((2, 2, tiles)),
            dma((2, 2, count)),
            dma((2,)),
        ],
        compiler_params=pltpu.CompilerParams(
            collective_id=0, has_side_effects=True, vmem_limit_bytes=56 << 20
        ),
    )(ranks, x_field, data, u_bases, v_bases)
    return pl.pallas_call(
        traces_kernel,
        name="traces",
        out_shape=jax.ShapeDtypeStruct((2 * count, share, points), f32),
        in_specs=[pl.BlockSpec(memory_space=pltpu.VMEM)] * 2,
        out_specs=pl.BlockSpec(memory_space=pltpu.VMEM),
        compiler_params=pltpu.CompilerParams(vmem_limit_bytes=32 << 20),
    )(spectra, onset)


def solution(mesh):
    in_specs = (
        P("freq", None, "tile", None),
        P("freq", None, "tile", None),
        P("freq", "tile", None, None, None, None),
        P("freq", None, "tile", None, None, None),
        P("freq", None, None),
        P(("tile", "freq"), None),
    )
    out_specs = P(None, ("tile", "freq"), None)
    return jax.shard_map(body, mesh=mesh, in_specs=in_specs, out_specs=out_specs, check_vma=False)
```

time: 141 us -> 95 us (0.67)
  Pallas kernels: 0 us -> 93.7 us
  waiting for transfers between devices: 44 us -> 0 us
  blocking collectives: 43.8 us -> 0 us
  local copies, waits for them, and re-layouts: 21.4 us -> 1.08 us
  starting transfers between devices: 16.7 us -> 0 us
  matrix products: 11.4 us -> 0 us
  other arithmetic: 3.14 us -> 0 us
    pallas_call x0 -> x2, Pallas kernels: none -> 93.7 us  [the longest x1 91.8 us: body(): pl.pallas_call(exchange_kernel, name='exchange', out_shape=jax.ShapeDtype...]
    all_to_all x2 -> x0, waiting for transfers between devices: 44 us -> none  [the longest x1 31.1 us: body(): lax.all_to_all(coeffs, 'tile', split_axis=0, concat_axis=0, tiled=True)]
    all_to_all x1 -> x0, blocking collectives: 43.8 us -> none  [body(): lax.all_to_all(adjoint, 'tile', split_axis=0, concat_axis=0, tiled=True)]
    all_to_all x2 -> x0, starting transfers between devices: 16.7 us -> none  [the longest x1 9.98 us: body(): lax.all_to_all(coeffs, 'tile', split_axis=0, concat_axis=0, tiled=True)]
    slice x3 -> x0, local copies, waits for them, and re-layouts: 12 us -> none  [the longest x1 6.93 us: body(): row_factors = u_bases[0, 0, :, :extent]]
    dot_general x6 -> x0, matrix products: 11.4 us -> none  [the longest x2 5.44 us: apply_factors(): jnp.einsum('nkps,nkpov->osv', factors, blended, preferred_element_type=jn...]
    unnamed x18 -> x4, local copies, waits for them, and re-layouts: 5.57 us -> 1.08 us
    broadcast_in_dim x1 -> x0, local copies, waits for them, and re-layouts: 1.78 us -> none  [body(): spectrum[None]]
  transfers between devices with their start and end apart: 2 -> 0, of which waited for: 2 -> 0; matrix products, arithmetic and copies ran while one was open for 5% -> 0% of each run, Pallas kernels for 0% -> 0%
where the time goes in v1:
time: 95 us; the launch traced here: 94.8 us
  Pallas kernels  93.7 us (99%)
  local copies, waits for them, and re-layouts  1.08 us (1%)
    pallas_call x1, Pallas kernels, body(): pl.pallas_call(exchange_kernel, name='exchange', out_shape=jax.ShapeDtype...  91.8 us

profile of v1, /device:TPU:1, one launch (start us, length us, event | category | flops | bytes accessed | tf_op | source)
XLA Modules:
  0.0 94.8 jit_solution(7356808105495652304)
XLA Ops:
  0.0 0.0 copy-start.1
  0.0 91.8 %exchange.1.s_ref = bf16[2,16,40,256]{3,2,1,0:T(8,128)(2,1)} custom-call(s32[1,16,16]{2,1,0:T(8,128)} %ranks_ref.1, bf16[1,2,640,256]{3,2,1,0:T(8,128)(2,1)} %x_hbm.1, bf16[1,2,640,256]{3,2,1,0:T(8,128)(2,1)} %d_hbm.1, bf16[1,1,16,128,2,640]{5,4,3,2,1,0:T(2,128)(2,1)} %u_hbm.1, bf16[1,16,1,128,2,640]{5,4,3,2,1,0:T(2,128)(2,1)} %v_hbm.1), custom_call_target="tpu_custom_call" | custom-call | tf_op jit(solution)/shard_map/exchange/pallas_call | solution.py:295
  91.9 0.0 copy-done.1
  91.9 0.0 copy-start
  91.9 1.1 %copy-done = bf16[2,16,40,256]{3,2,1,0:T(8,128)(2,1)S(1)} copy-done((bf16[2,16,40,256]{3,2,1,0:T(8,128)(2,1)S(1)}, bf16[2,16,40,256]{3,2,1,0:T(8,128)(2,1)}, u32[]{:S(2)}) %copy-start) | copy-done | bytes 655384
  93.0 1.8 %traces.1 = f32[32,40,256]{2,1,0:T(8,128)} custom-call(bf16[2,16,40,256]{3,2,1,0:T(8,128)(2,1)S(1)} %copy-done, s32[40,256]{1,0:T(8,128)S(1)} %copy-done.1), custom_call_target="tpu_custom_call" | custom-call | tf_op jit(solution)/shard_map/traces/pallas_call | solution.py:328
Async XLA Ops:
  0.0 91.9 %copy-start.1 = (s32[40,256]{1,0:T(8,128)S(1)}, s32[40,256]{1,0:T(8,128)}, u32[]{:S(2)}) copy-start(s32[40,256]{1,0:T(8,128)} %onset_ref.1) | copy-start | bytes 122884
  91.9 1.1 %copy-start = (bf16[2,16,40,256]{3,2,1,0:T(8,128)(2,1)S(1)}, bf16[2,16,40,256]{3,2,1,0:T(8,128)(2,1)}, u32[]{:S(2)}) copy-start(bf16[2,16,40,256]{3,2,1,0:T(8,128)(2,1)} %exchange.1.s_ref) | copy-start | bytes 1966084

commit v2 on v0

v2 whole, which is shorter than its diff:
```python
import math

import jax
import jax.numpy as jnp
from jax import lax
from jax.experimental import pallas as pl
from jax.experimental.pallas import tpu as pltpu
from jax.sharding import PartitionSpec as P

RMAX = 96
HALF = 128
TILES = 16
LAST = TILES - 1
FREQS = 16
MESH = pl.DeviceIdType.MESH
CONTRACT_ROWS = (((0,), (0,)), ((), ()))
FREQ_ORDER = (10, 6, 9, 11, 14, 2, 8, 5, 7, 13, 15, 1, 3, 4, 12)


def weighted(terms):
    value = None
    for factor, term in terms:
        if abs(factor) < 1e-12:
            continue
        product = term * jnp.float32(factor)
        value = product if value is None else value + product
    return value


def traces(real, imag, store):
    count = len(real)
    period = 2 * count
    scale = 1.0 / math.sqrt(count)
    for t in range(count // 2 + 1):
        angles = [2 * math.pi * (((f + 1) * t) % period) / period for f in range(count)]
        cosine = [scale * math.cos(a) for a in angles]
        sine = [scale * math.sin(a) for a in angles]
        sums = []
        for factors, values in ((cosine, real), (sine, imag)):
            for start in (0, 1):
                part = weighted([(factors[f], values[f]) for f in range(start, count, 2)])
                sums.append(jnp.zeros_like(real[0]) if part is None else part)
        odd_c, even_c, odd_s, even_s = sums
        sum_c, difference_c, sum_s, difference_s = even_c + odd_c, even_c - odd_c, even_s + odd_s, even_s - odd_s
        store(t, sum_c - sum_s)
        if t < count - t:
            store(count - t, difference_c + difference_s)
        if 0 < t:
            store(period - t, sum_c + sum_s)
            if count + t < period - t:
                store(count + t, difference_c - difference_s)


def half_traces(received, onset_ref, target, half, block):
    rows = pl.ds(pl.multiple_of(block * 8, 8), 8)
    onset = onset_ref[rows, pl.ds(half * HALF, HALF)]
    count = received.shape[0]
    real = [received[f, rows, pl.ds(0, HALF)].astype(jnp.float32) for f in range(count)]
    imag = [received[f, rows, pl.ds(HALF, HALF)].astype(jnp.float32) for f in range(count)]

    def store(time, value):
        target[time, rows, :] = jnp.where(onset <= time, value, 0.0)

    traces(real, imag, store)


def exchange_kernel(
    ranks_ref, onset_ref, x_hbm, d_hbm, u_hbm, v_hbm, f_recv, first_ref,
    x_mat, x_rot, d_mat, v_raw, u_raw, v_re, v_im, u_re, u_im, total,
    c_send, c_recv, a_send, a_recv, f_send, f_first,
    load_sem, v_sem, u_sem, c_sems, a_sems, f_sems,
):
    freq = lax.axis_index("freq")
    tile = lax.axis_index("tile")
    chip, core = lax.div(tile, 2), lax.rem(tile, 2)
    freq_y, freq_x = lax.div(freq, 4), lax.rem(freq, 4)

    def tile_at(group, index, sign):
        chips = 4 + group if index < 2 else 3 - group
        peer = lax.rem(chip + sign * chips + 8, 8)
        return peer * 2 + (core if index % 2 else 1 - core)

    def freq_at(offset):
        return lax.rem(freq_y + offset // 4, 4) * 4 + lax.rem(freq_x + offset % 4, 4)

    def field_copy(source, target, half, part, index):
        return pltpu.make_async_copy(
            source.at[0, part, :, pl.ds(half * HALF, HALF)],
            target.at[half, :, pl.ds(part * HALF, HALF)],
            load_sem.at[index, half, part],
        )

    def load_field(source, target, half, index):
        for part in range(2):
            field_copy(source, target, half, part, index).start()

    def wait_field(source, target, half, index):
        for part in range(2):
            field_copy(source, target, half, part, index).wait()

    def v_copy(group, index):
        slot = 4 * group + index
        return pltpu.make_async_copy(
            v_hbm.at[0, tile_at(group, index, 1), 0, pl.ds(0, RMAX)], v_raw.at[slot], v_sem.at[slot]
        )

    def u_copy(group, index):
        slot = 4 * group + index
        return pltpu.make_async_copy(
            u_hbm.at[0, 0, tile_at(group, index, -1), pl.ds(0, RMAX)], u_raw.at[slot], u_sem.at[slot]
        )

    load_field(x_hbm, x_mat, 0, 0)
    for index in range(4):
        v_copy(0, index).start()

    barrier = pltpu.get_barrier_semaphore()
    for slot in range(LAST):
        pl.semaphore_signal(
            barrier, inc=1, device_id=(freq, tile_at(slot // 4, slot % 4, 1)), device_id_type=MESH
        )
    for offset in FREQ_ORDER:
        pl.semaphore_signal(barrier, inc=1, device_id=(freq_at(offset), tile), device_id_type=MESH)

    for group in range(1, 4):
        for index in range(4):
            v_copy(group, index).start()

    rows = lax.broadcasted_iota(jnp.int32, (2 * RMAX, 2 * RMAX), 0)
    columns = lax.broadcasted_iota(jnp.int32, (2 * RMAX, 2 * RMAX), 1)
    wanted = jnp.where(rows < RMAX, 2 * rows, 2 * (rows - RMAX) + 1)
    separate = jnp.where(columns == wanted, 1.0, 0.0).astype(jnp.bfloat16)
    levels = lax.broadcasted_iota(jnp.int32, (RMAX, 2 * HALF), 0)

    def piece(slot):
        return pl.ds(pl.multiple_of(slot * RMAX, RMAX), RMAX)

    def pieces(group):
        return pl.ds(pl.multiple_of(group * 4 * RMAX, 4 * RMAX), 4 * RMAX)

    def prepare(slot, raw, real, imag):
        interleaved = raw[slot].reshape(2 * RMAX, raw.shape[-1])
        parts = jnp.dot(separate, interleaved, preferred_element_type=jnp.float32).astype(jnp.bfloat16)
        real[piece(slot)] = parts[:RMAX]
        imag[piece(slot)] = parts[RMAX:]

    def prepare_v(group):
        for index in range(4):
            v_copy(group, index).wait()
            prepare(4 * group + index, v_raw, v_re, v_im)

    def prepare_u(group):
        for index in range(4):
            u_copy(group, index).wait()
            prepare(4 * group + index, u_raw, u_re, u_im)

    def rotated(field):
        return jnp.concatenate([field[:, HALF:], -field[:, :HALF]], axis=1)

    def conj_apply(real, imag, half, group, send, ranks):
        value = jnp.dot(real[pieces(group)], x_mat[half], preferred_element_type=jnp.float32)
        value += jnp.dot(imag[pieces(group)], x_rot[half], preferred_element_type=jnp.float32)
        for index in range(4):
            part = value[index * RMAX:(index + 1) * RMAX]
            part = jnp.where(levels < ranks(index), part, 0.0)
            send[half, piece(4 * group + index)] = part.astype(jnp.bfloat16)

    def c_copy(half, group, index):
        slot = 4 * group + index
        return pltpu.make_async_remote_copy(
            src_ref=c_send.at[half, piece(slot)], dst_ref=c_recv.at[half, piece(slot)],
            send_sem=c_sems.at[0, half, slot], recv_sem=c_sems.at[1, half, slot],
            device_id=(freq, tile_at(group, index, 1)), device_id_type=MESH,
        )

    def a_copy(half, group, index):
        slot = 4 * group + index
        return pltpu.make_async_remote_copy(
            src_ref=a_send.at[half, piece(slot)], dst_ref=a_recv.at[half, piece(slot)],
            send_sem=a_sems.at[0, half, slot], recv_sem=a_sems.at[1, half, slot],
            device_id=(freq, tile_at(group, index, -1)), device_id_type=MESH,
        )

    def f_copy(half, offset):
        return pltpu.make_async_remote_copy(
            src_ref=f_send.at[half, offset], dst_ref=(f_recv if half else f_first).at[freq],
            send_sem=f_sems.at[0, half, offset], recv_sem=f_sems.at[1, half, offset],
            device_id=(freq_at(offset), tile), device_id_type=MESH,
        )

    def each_remote(action):
        def step(group, carry):
            for index in range(4):
                action(group, index)
            return carry

        lax.fori_loop(0, 3, step, 0)
        for index in range(3):
            action(3, index)

    def coefficients(half, group):
        conj_apply(v_re, v_im, half, group, c_send, lambda index: ranks_ref[0, tile_at(group, index, 1), tile])

    def adjoint(half, group):
        conj_apply(u_re, u_im, half, group, a_send, lambda index: ranks_ref[0, tile, tile_at(group, index, -1)])

    def keep_own(send, receive, half):
        receive[half, piece(LAST)] = send[half, piece(LAST)]

    wait_field(x_hbm, x_mat, 0, 0)
    x_rot[0] = rotated(x_mat[0])
    prepare_v(0)
    coefficients(0, 0)
    pl.semaphore_wait(barrier, LAST + len(FREQ_ORDER))
    for index in range(4):
        c_copy(0, 0, index).start()

    load_field(x_hbm, x_mat, 1, 0)
    for half in range(2):
        load_field(d_hbm, d_mat, half, 1)
    for group in range(4):
        for index in range(4):
            u_copy(group, index).start()

    def first_step(group, carry):
        prepare_v(group)
        coefficients(0, group)
        for index in range(4):
            c_copy(0, group, index).start()
        return carry

    lax.fori_loop(1, 3, first_step, 0)
    prepare_v(3)
    coefficients(0, 3)
    for index in range(3):
        c_copy(0, 3, index).start()
    keep_own(c_send, c_recv, 0)

    wait_field(x_hbm, x_mat, 1, 0)
    x_rot[1] = rotated(x_mat[1])

    def second_step(group, carry):
        coefficients(1, group)
        prepare_u(group)
        return carry

    lax.fori_loop(0, 4, second_step, 0)
    keep_own(c_send, c_recv, 1)

    def send_second(group, index):
        c_copy(0, group, index).wait_send()
        c_copy(1, group, index).start()

    each_remote(send_second)

    def gather(half, copy, received, real, imag):
        def add(group):
            at = pieces(group)
            weights = received[half, at]
            partner = jnp.concatenate([-weights[:, HALF:], weights[:, :HALF]], axis=1)
            value = lax.dot_general(real[at], weights, CONTRACT_ROWS, preferred_element_type=jnp.float32)
            total[...] += value + lax.dot_general(
                imag[at], partner, CONTRACT_ROWS, preferred_element_type=jnp.float32
            )

        def step(group, carry):
            for index in range(4):
                copy(half, group, index).wait_recv()
            add(group)
            return carry

        lax.fori_loop(0, 3, step, 0)
        for index in range(3):
            copy(half, 3, index).wait_recv()
        add(3)

    for half in range(2):
        wait_field(d_hbm, d_mat, half, 1)
        total[...] = -d_mat[half].astype(jnp.float32)
        gather(half, c_copy, c_recv, u_re, u_im)
        x_mat[half] = total[...].astype(jnp.bfloat16)
        x_rot[half] = rotated(x_mat[half])

        def adjoint_step(group, carry):
            adjoint(half, group)
            for index in range(4):
                (a_copy(0, group, index) if half else c_copy(1, group, index)).wait_send()
                a_copy(half, group, index).start()
            return carry

        lax.fori_loop(0, 3, adjoint_step, 0)
        adjoint(half, 3)
        for index in range(3):
            (a_copy(0, 3, index) if half else c_copy(1, 3, index)).wait_send()
            a_copy(half, 3, index).start()
        keep_own(a_send, a_recv, half)

    share = f_recv.shape[1]
    for half in range(2):
        total[...] = jnp.zeros_like(total)
        gather(half, a_copy, a_recv, v_re, v_im)

        def spectrum(peer):
            return total[pl.ds(pl.multiple_of(peer * share, 8), share)].astype(jnp.bfloat16)

        for offset in FREQ_ORDER:
            f_send[half, offset] = spectrum(freq_at(offset))
            f_copy(half, offset).start()
        (f_recv if half else f_first)[freq] = spectrum(freq)
        if half == 0:
            for offset in FREQ_ORDER:
                f_copy(0, offset).wait()

            def trace_step(block, carry):
                half_traces(f_first, onset_ref, first_ref, 0, block)
                return carry

            lax.fori_loop(0, share // 8, trace_step, 0)

    each_remote(lambda group, index: a_copy(1, group, index).wait_send())
    for offset in FREQ_ORDER:
        f_copy(1, offset).wait()


def finish_kernel(first_ref, received, onset_ref, out_ref, second, sems):
    share = second.shape[1]
    first = pltpu.make_async_copy(first_ref, out_ref.at[:, :, pl.ds(0, HALF)], sems.at[0])
    first.start()
    copies = []
    for block in range(share // 8):
        half_traces(received, onset_ref, second, 1, block)
        rows = pl.ds(block * 8, 8)
        copy = pltpu.make_async_copy(
            second.at[:, rows], out_ref.at[:, rows, pl.ds(HALF, HALF)], sems.at[1 + block]
        )
        copy.start()
        copies.append(copy)
    first.wait()
    for copy in copies:
        copy.wait()


def body(x_field, data, u_bases, v_bases, ranks, onset):
    stations, points = x_field.shape[2:]
    share = stations // FREQS
    times = 2 * FREQS
    bf16, f32 = jnp.bfloat16, jnp.float32
    anywhere = pl.BlockSpec(memory_space=pl.ANY)
    vmem = pl.BlockSpec(memory_space=pltpu.VMEM)
    dma = pltpu.SemaphoreType.DMA
    field = pltpu.VMEM((2, stations, 2 * HALF), bf16)
    raw = pltpu.VMEM((TILES, RMAX, 2, stations), bf16)
    basis = pltpu.VMEM((TILES * RMAX, stations), bf16)
    message = pltpu.VMEM((2, TILES * RMAX, 2 * HALF), bf16)
    received, first = pl.pallas_call(
        exchange_kernel,
        name="exchange",
        out_shape=(
            pltpu.VMEM((FREQS, share, 2 * HALF), bf16),
            pltpu.VMEM((times, share, HALF), f32),
        ),
        in_specs=[pl.BlockSpec(memory_space=pltpu.SMEM), vmem] + [anywhere] * 4,
        out_specs=(vmem, vmem),
        scratch_shapes=[
            field, field, field, raw, raw, basis, basis, basis, basis,
            pltpu.VMEM((stations, 2 * HALF), f32),
            message, message, message, message,
            pltpu.VMEM((2, FREQS, share, 2 * HALF), bf16),
            pltpu.VMEM((FREQS, share, 2 * HALF), bf16),
            dma((2, 2, 2)),
            dma((TILES,)),
            dma((TILES,)),
            dma((2, 2, TILES)),
            dma((2, 2, TILES)),
            dma((2, 2, FREQS)),
        ],
        compiler_params=pltpu.CompilerParams(
            collective_id=0, has_side_effects=True, vmem_limit_bytes=56 << 20
        ),
    )(ranks, onset, x_field, data, u_bases, v_bases)
    return pl.pallas_call(
        finish_kernel,
        name="finish",
        out_shape=jax.ShapeDtypeStruct((times, share, points), f32),
        in_specs=[vmem] * 3,
        out_specs=anywhere,
        scratch_shapes=[pltpu.VMEM((times, share, HALF), f32), dma((1 + share // 8,))],
        compiler_params=pltpu.CompilerParams(vmem_limit_bytes=32 << 20),
    )(first, received, onset)


def solution(mesh):
    in_specs = (
        P("freq", None, "tile", None),
        P("freq", None, "tile", None),
        P("freq", "tile", None, None, None, None),
        P("freq", None, "tile", None, None, None),
        P("freq", None, None),
        P(("tile", "freq"), None),
    )
    out_specs = P(None, ("tile", "freq"), None)
    return jax.shard_map(body, mesh=mesh, in_specs=in_specs, out_specs=out_specs, check_vma=False)
```

time: 141 us -> 90.5 us (0.64)
  Pallas kernels: 0 us -> 89.5 us
  waiting for transfers between devices: 44 us -> 0 us
  blocking collectives: 43.8 us -> 0 us
  local copies, waits for them, and re-layouts: 21.4 us -> 0.01 us
  starting transfers between devices: 16.7 us -> 0 us
  matrix products: 11.4 us -> 0 us
  other arithmetic: 3.14 us -> 0 us
    pallas_call x0 -> x2, Pallas kernels: none -> 89.5 us  [the longest x1 88.4 us: body(): pl.pallas_call(exchange_kernel, name='exchange', out_shape=(pltpu.VMEM((F...]
    all_to_all x2 -> x0, waiting for transfers between devices: 44 us -> none  [the longest x1 31.1 us: body(): lax.all_to_all(coeffs, 'tile', split_axis=0, concat_axis=0, tiled=True)]
    all_to_all x1 -> x0, blocking collectives: 43.8 us -> none  [body(): lax.all_to_all(adjoint, 'tile', split_axis=0, concat_axis=0, tiled=True)]
    all_to_all x2 -> x0, starting transfers between devices: 16.7 us -> none  [the longest x1 9.98 us: body(): lax.all_to_all(coeffs, 'tile', split_axis=0, concat_axis=0, tiled=True)]
    slice x3 -> x0, local copies, waits for them, and re-layouts: 12 us -> none  [the longest x1 6.93 us: body(): row_factors = u_bases[0, 0, :, :extent]]
    dot_general x6 -> x0, matrix products: 11.4 us -> none  [the longest x2 5.44 us: apply_factors(): jnp.einsum('nkps,nkpov->osv', factors, blended, preferred_element_type=jn...]
    unnamed x18 -> x2, local copies, waits for them, and re-layouts: 5.57 us -> 0.01 us
    broadcast_in_dim x1 -> x0, local copies, waits for them, and re-layouts: 1.78 us -> none  [body(): spectrum[None]]
  transfers between devices with their start and end apart: 2 -> 0, of which waited for: 2 -> 0; matrix products, arithmetic and copies ran while one was open for 5% -> 0% of each run, Pallas kernels for 0% -> 0%
where the time goes in v2:
time: 90.5 us; the launch traced here: 89.5 us
  Pallas kernels  89.5 us (99%)
    pallas_call x1, Pallas kernels, body(): pl.pallas_call(exchange_kernel, name='exchange', out_shape=(pltpu.VMEM((F...  88.4 us

profile of v2, /device:TPU:1, one launch (start us, length us, event | category | flops | bytes accessed | tf_op | source)
XLA Modules:
  0.0 89.5 jit_solution(13366136764868495753)
XLA Ops:
  0.0 0.0 copy-start
  0.0 88.4 %exchange.1 = (bf16[16,40,256]{2,1,0:T(8,128)(2,1)S(1)}, f32[32,40,128]{2,1,0:T(8,128)S(1)}) custom-call(s32[1,16,16]{2,1,0:T(8,128)} %ranks_ref.1, s32[40,256]{1,0:T(8,128)} %onset_ref.3, bf16[1,2,640,256]{3,2,1,0:T(8,128)(2,1)} %x_hbm.1, bf16[1,2,640,256]{3,2,1,0:T(8,128)(2,1)} %d_hbm.1, bf16[1,1,16,128,2,640]{5,4,3,2,1,0:T(2,128)(2,1)} %u_hbm.1, ...), custom_call_target="tpu_custom_call" | custom-call | tf_op jit(solution)/shard_map/exchange/pallas_call | solution.py:355
  88.4 0.0 copy-done
  88.4 1.1 %finish.1 = f32[32,40,256]{2,1,0:T(8,128)} custom-call(f32[32,40,128]{2,1,0:T(8,128)S(1)} %get-tuple-element.7.first_ref, bf16[16,40,256]{2,1,0:T(8,128)(2,1)S(1)} %get-tuple-element.8.received, s32[40,256]{1,0:T(8,128)S(1)} %copy-done), custom_call_target="tpu_custom_call" | custom-call | tf_op jit(solution)/shard_map/finish/pallas_call | solution.py:381
Async XLA Ops:
  0.0 88.4 %copy-start = (s32[40,256]{1,0:T(8,128)S(1)}, s32[40,256]{1,0:T(8,128)}, u32[]{:S(2)}) copy-start(s32[40,256]{1,0:T(8,128)} %onset_ref.3) | copy-start | bytes 122884

commit v3 on v2

--- a/solution.py
+++ b/solution.py
@@ -76,7 +76,7 @@
     freq_y, freq_x = lax.div(freq, 4), lax.rem(freq, 4)
 
     def tile_at(group, index, sign):
-        chips = 4 + group if index < 2 else 3 - group
+        chips = 7 - group if index < 2 else lax.rem(group + 1, 4)
         peer = lax.rem(chip + sign * chips + 8, 8)
         return peer * 2 + (core if index % 2 else 1 - core)
 
@@ -248,7 +248,6 @@
     keep_own(c_send, c_recv, 1)
 
     def send_second(group, index):
-        c_copy(0, group, index).wait_send()
         c_copy(1, group, index).start()
 
     each_remote(send_second)
@@ -284,14 +283,12 @@
         def adjoint_step(group, carry):
             adjoint(half, group)
             for index in range(4):
-                (a_copy(0, group, index) if half else c_copy(1, group, index)).wait_send()
                 a_copy(half, group, index).start()
             return carry
 
         lax.fori_loop(0, 3, adjoint_step, 0)
         adjoint(half, 3)
         for index in range(3):
-            (a_copy(0, 3, index) if half else c_copy(1, 3, index)).wait_send()
             a_copy(half, 3, index).start()
         keep_own(a_send, a_recv, half)
 
@@ -317,7 +314,9 @@
 
             lax.fori_loop(0, share // 8, trace_step, 0)
 
-    each_remote(lambda group, index: a_copy(1, group, index).wait_send())
+    for copy in (c_copy, a_copy):
+        for half in range(2):
+            each_remote(lambda group, index: copy(half, group, index).wait_send())
     for offset in FREQ_ORDER:
         f_copy(1, offset).wait()
 

time: 90.5 us -> 90.1 us (level)
  no operation moved by 1% of the time
where the time goes in v3:
time: 90.1 us; the launch traced here: 88.8 us
  Pallas kernels  88.8 us (99%)
    pallas_call x1, Pallas kernels, body(): pl.pallas_call(exchange_kernel, name='exchange', out_shape=(pltpu.VMEM((F...  87.7 us

profile of v3, /device:TPU:1, one launch (start us, length us, event | category | flops | bytes accessed | tf_op | source)
XLA Modules:
  0.0 88.8 jit_solution(5366857744034500345)
XLA Ops:
  0.0 0.0 copy-start
  0.0 87.7 %exchange.1 = (bf16[16,40,256]{2,1,0:T(8,128)(2,1)S(1)}, f32[32,40,128]{2,1,0:T(8,128)S(1)}) custom-call(s32[1,16,16]{2,1,0:T(8,128)} %ranks_ref.1, s32[40,256]{1,0:T(8,128)} %onset_ref.3, bf16[1,2,640,256]{3,2,1,0:T(8,128)(2,1)} %x_hbm.1, bf16[1,2,640,256]{3,2,1,0:T(8,128)(2,1)} %d_hbm.1, bf16[1,1,16,128,2,640]{5,4,3,2,1,0:T(2,128)(2,1)} %u_hbm.1, ...), custom_call_target="tpu_custom_call" | custom-call | tf_op jit(solution)/shard_map/exchange/pallas_call | solution.py:354
  87.7 0.0 copy-done
  87.7 1.1 %finish.1 = f32[32,40,256]{2,1,0:T(8,128)} custom-call(f32[32,40,128]{2,1,0:T(8,128)S(1)} %get-tuple-element.7.first_ref, bf16[16,40,256]{2,1,0:T(8,128)(2,1)S(1)} %get-tuple-element.8.received, s32[40,256]{1,0:T(8,128)S(1)} %copy-done), custom_call_target="tpu_custom_call" | custom-call | tf_op jit(solution)/shard_map/finish/pallas_call | solution.py:380
Async XLA Ops:
  0.0 87.7 %copy-start = (s32[40,256]{1,0:T(8,128)S(1)}, s32[40,256]{1,0:T(8,128)}, u32[]{:S(2)}) copy-start(s32[40,256]{1,0:T(8,128)} %onset_ref.3) | copy-start | bytes 122884

commit v4 on v3

--- a/solution.py
+++ b/solution.py
@@ -252,9 +252,9 @@
 
     each_remote(send_second)
 
-    def gather(half, copy, received, real, imag):
-        def add(group):
-            at = pieces(group)
+    def gather(half, copy, received, real, imag, split=False):
+        def add(slot, count=4):
+            at = pl.ds(pl.multiple_of(slot * RMAX, 2 * RMAX), count * RMAX)
             weights = received[half, at]
             partner = jnp.concatenate([-weights[:, HALF:], weights[:, :HALF]], axis=1)
             value = lax.dot_general(real[at], weights, CONTRACT_ROWS, preferred_element_type=jnp.float32)
@@ -265,13 +265,16 @@
         def step(group, carry):
             for index in range(4):
                 copy(half, group, index).wait_recv()
-            add(group)
+            add(4 * group)
             return carry
 
+        if split:
+            copy(half, 3, 2).wait_recv()
+            add(14, 2)
         lax.fori_loop(0, 3, step, 0)
-        for index in range(3):
+        for index in range(2 if split else 3):
             copy(half, 3, index).wait_recv()
-        add(3)
+        add(12, 2 if split else 4)
 
     for half in range(2):
         wait_field(d_hbm, d_mat, half, 1)
@@ -295,7 +298,7 @@
     share = f_recv.shape[1]
     for half in range(2):
         total[...] = jnp.zeros_like(total)
-        gather(half, a_copy, a_recv, v_re, v_im)
+        gather(half, a_copy, a_recv, v_re, v_im, half == 1)
 
         def spectrum(peer):
             return total[pl.ds(pl.multiple_of(peer * share, 8), share)].astype(jnp.bfloat16)

time: 90.1 us -> 89.9 us (level)
  no operation moved by 1% of the time
where the time goes in v4:
time: 89.9 us; the launch traced here: 88.6 us
  Pallas kernels  88.6 us (99%)
    pallas_call x1, Pallas kernels, body(): pl.pallas_call(exchange_kernel, name='exchange', out_shape=(pltpu.VMEM((F...  87.5 us

profile of v4, /device:TPU:1, one launch (start us, length us, event | category | flops | bytes accessed | tf_op | source)
XLA Modules:
  0.0 88.6 jit_solution(15237606862021826711)
XLA Ops:
  0.0 0.0 copy-start
  0.0 87.5 %exchange.1 = (bf16[16,40,256]{2,1,0:T(8,128)(2,1)S(1)}, f32[32,40,128]{2,1,0:T(8,128)S(1)}) custom-call(s32[1,16,16]{2,1,0:T(8,128)} %ranks_ref.1, s32[40,256]{1,0:T(8,128)} %onset_ref.3, bf16[1,2,640,256]{3,2,1,0:T(8,128)(2,1)} %x_hbm.1, bf16[1,2,640,256]{3,2,1,0:T(8,128)(2,1)} %d_hbm.1, bf16[1,1,16,128,2,640]{5,4,3,2,1,0:T(2,128)(2,1)} %u_hbm.1, ...), custom_call_target="tpu_custom_call" | custom-call | tf_op jit(solution)/shard_map/exchange/pallas_call | solution.py:357
  87.5 0.0 copy-done
  87.5 1.1 %finish.1 = f32[32,40,256]{2,1,0:T(8,128)} custom-call(f32[32,40,128]{2,1,0:T(8,128)S(1)} %get-tuple-element.7.first_ref, bf16[16,40,256]{2,1,0:T(8,128)(2,1)S(1)} %get-tuple-element.8.received, s32[40,256]{1,0:T(8,128)S(1)} %copy-done), custom_call_target="tpu_custom_call" | custom-call | tf_op jit(solution)/shard_map/finish/pallas_call | solution.py:383
Async XLA Ops:
  0.0 87.5 %copy-start = (s32[40,256]{1,0:T(8,128)S(1)}, s32[40,256]{1,0:T(8,128)}, u32[]{:S(2)}) copy-start(s32[40,256]{1,0:T(8,128)} %onset_ref.3) | copy-start | bytes 122884
